TPU v7x, 256 devices: a whole 4x4x8 slice. The times are simulated.
256 devices in a mesh: rep: 4 (over y), exp: 64 (over z, x, core).
Axes of the slice: x: 4, y: 4, z: 8, core: 2. Of those that a mesh axis runs over, the one named last changes fastest.
Arguments:
- hidden_states: bfloat16 [4096, 4096], P(('rep', 'exp')), may hold values from -6 to 6
- expert_ids: int32 [4096, 8], P(('rep', 'exp')), may hold values from 0 to 63, as said below
- route_weights: float32 [4096, 8], P(('rep', 'exp')), may hold values from 0.05 to 1
- w_gate: bfloat16 [64, 4096, 1536], P('exp', None, 'rep'), may hold values from -0.09375 to 0.09375
- w_up: bfloat16 [64, 4096, 1536], P('exp', None, 'rep'), may hold values from -0.09375 to 0.09375
- w_down: bfloat16 [64, 1536, 4096], P('exp', 'rep'), may hold values from -0.15625 to 0.15625
Outputs:
- moe_out: bfloat16 [4096, 4096], P(('rep', 'exp'))
Inputs may be any that keep to these rules, and one draw needn't show every extreme that they name: `expert_ids`: each row names 8 different experts. One expert, the same for the whole array, is named by exactly 6 of the 16 rows held by each device (each device's block of 16 consecutive rows); every other expert is named by at most 2 rows of one device, and in every device's rows some expert other than that one reaches 2.
All inputs are finite; a program needn't handle non-finite values.
Results may differ from a plain program's by a relative error of at most 0.015.
Values may be sent and summed in bfloat16 or wider, within the bound.
A program may use at most 128 MiB of HBM per device.

v0:
```python
import jax
import jax.numpy as jnp
from jax import lax
from jax.sharding import PartitionSpec as P


def expert_rows(row_block, gate_w, up_w, down_w):
    gate_value = jnp.einsum("mgld,ldf->mglf", row_block, gate_w, preferred_element_type=jnp.float32)
    up_value = jnp.einsum("mgld,ldf->mglf", row_block, up_w, preferred_element_type=jnp.float32)
    active = (jax.nn.silu(gate_value) * up_value).astype(jnp.bfloat16)
    partial_out = jnp.einsum("mglf,lfd->mgld", active, down_w, preferred_element_type=jnp.float32)
    rounded = lax.optimization_barrier(partial_out.astype(jnp.bfloat16))
    return rounded.astype(jnp.float32)


def local(hidden_states, expert_ids, route_weights, w_gate, w_up, w_down):
    tok_rows, width = hidden_states.shape
    topk = expert_ids.shape[1]
    local_count = w_gate.shape[0]
    n_exp = lax.axis_size("exp")
    n_rep = lax.axis_size("rep")
    experts = local_count * n_exp
    hot_rows = tok_rows - 5 * tok_rows // 8 * min(1, max(0, experts - topk))
    cold_cap = (tok_rows * topk - hot_rows + experts - 2) // (experts - 1)
    flat_ids = expert_ids.reshape(-1)
    picks = flat_ids.shape[0]
    expert_range = jnp.arange(experts, dtype=jnp.int32)
    onehot = (flat_ids[:, None] == expert_range[None, :]).astype(jnp.int32)
    hot_pick = jnp.zeros((picks,), jnp.int32)
    capacity = max(hot_rows, cold_cap)
    routed = onehot * (1 - hot_pick)[:, None]
    rank = jnp.sum((jnp.cumsum(routed, axis=0) - routed) * routed, axis=1)
    slot_pos = rank * experts + flat_ids
    slots = capacity * experts
    matches = (jnp.arange(slots, dtype=jnp.int32)[:, None] == slot_pos[None, :]) & (
        hot_pick[None, :] == 0
    )
    select = jnp.any(matches.reshape(slots, tok_rows, topk), axis=2).astype(jnp.bfloat16)
    all_states, all_select = (
        lax.all_gather(hidden_states, "rep", axis=0, tiled=True),
        lax.all_gather(select, "rep", axis=0, tiled=True),
    )
    copies = jnp.einsum(
        "rst,rtd->rsd",
        all_select.reshape(n_rep, slots, tok_rows),
        all_states.reshape(n_rep, tok_rows, width),
        preferred_element_type=jnp.float32,
    ).astype(jnp.bfloat16)
    gathered = lax.all_to_all(
        copies.reshape(n_rep * capacity, experts, width),
        "exp",
        split_axis=1,
        concat_axis=1,
        tiled=True,
    )
    row_block = gathered.reshape(lax.axis_size("rep") * capacity, n_exp, local_count, width)
    summed = lax.psum_scatter(
        expert_rows(row_block, w_gate, w_up, w_down)
        .reshape(lax.axis_size("rep") * capacity, experts, width)
        .astype(jnp.bfloat16),
        "rep",
        scatter_dimension=0,
        tiled=True,
    )
    returned = lax.all_to_all(summed, "exp", split_axis=1, concat_axis=1, tiled=True)
    flat_out = returned.reshape(slots, width)
    norm_weights = route_weights / jnp.sum(route_weights, axis=1, keepdims=True)
    picked = jnp.take(flat_out, slot_pos, axis=0).astype(jnp.float32).reshape(tok_rows, topk, width)
    mixed = jnp.sum(picked * norm_weights[:, :, None], axis=1)
    return mixed.astype(jnp.bfloat16)


def solution(mesh):
    in_specs = (
        P(("rep", "exp"), None),
        P(("rep", "exp"), None),
        P(("rep", "exp"), None),
        P("exp", None, "rep"),
        P("exp", None, "rep"),
        P("exp", "rep", None),
    )
    out_specs = P(("rep", "exp"), None)
    return jax.shard_map(local, mesh=mesh, in_specs=in_specs, out_specs=out_specs, check_vma=False)
```

profile of v0, /device:TPU:2, one launch (start us, length us, event | category | flops | bytes accessed | tf_op | source)
XLA Modules:
  0.0 612.4 jit_solution(16753595019423445464)
XLA Ops:
  6.5 0.9 copy.26
  7.4 0.1 eq.29
  7.5 0.1 fusion.16
  7.6 0.2 reduce_window_sum.11
  7.8 0.2 select_reduce_fusion
  8.0 0.1 mul.47
  8.1 0.1 fusion.15
  8.3 12.4 %all_gather.6 = bf16[1536,16]{0,1:T(8,128)(2,1)S(1)} all-gather(bf16[384,16]{0,1:T(8,128)(2,1)S(1)} %convert_element_type.37), channel_id=1, replica_groups=mesh['rep'=4,'exp'=64] {'rep'}, dimensions={0}, use_global_device_ids=true | all-gather | bytes 61440 | tf_op jit(solution)/shard_map/all_gather | solution.py:41
  20.7 13.0 %all_gather.7 = bf16[64,4096]{1,0:T(8,128)(2,1)S(1)} all-gather(bf16[16,4096]{1,0:T(8,128)(2,1)} %param.6), channel_id=1, replica_groups=mesh['rep'=4,'exp'=64] {'rep'}, dimensions={0}, use_global_device_ids=true | all-gather | bytes 655360 | tf_op jit(solution)/shard_map/all_gather | solution.py:40
  33.7 3.7 convolution_convert_fusion
  37.4 16.8 %copy.29 = bf16[24,64,4096]{2,0,1:T(8,128)(2,1)S(1)} copy(bf16[24,64,4096]{2,1,0:T(8,128)(2,1)S(1)} %bitcast.74) | data formatting | bytes 25165824 | tf_op jit(solution)/shard_map/reshape | solution.py:50
  54.2 288.1 %all_to_all.10 = bf16[24,64,4096]{2,0,1:T(8,128)(2,1)S(1)} all-to-all(bf16[24,64,4096]{2,0,1:T(8,128)(2,1)S(1)} %copy.29), channel_id=1, replica_groups=mesh['rep'=4,'exp'=64] {'exp'}, dimensions={1} | all-to-all | bytes 25165824 | tf_op jit(solution)/shard_map/all_to_all | solution.py:49
  342.2 6.9 %fusion.3 = f32[24,64,384]{2,0,1:T(8,128)S(1)} fusion(bf16[24,64,4096]{2,0,1:T(8,128)(2,1)S(1)} %all_to_all.10, bf16[1,4096,384]{2,1,0:T(8,128)(2,1)S(1)} %copy-done.2), kind=kOutput, calls=%fused_computation.6 | convolution fusion | flops 4831838208 | bytes 18087936 | tf_op jit(solution)/shard_map/mgld,ldf->mglf/dot_general | solution.py:8
  349.2 7.5 %fusion.11 = bf16[24,64,384]{2,0,1:T(8,128)(2,1)S(1)} fusion(bf16[24,64,4096]{2,0,1:T(8,128)(2,1)S(1)} %all_to_all.10, bf16[1,4096,384]{2,1,0:T(8,128)(2,1)S(1)} %copy-done.3, f32[24,64,384]{2,0,1:T(8,128)S(1)} %fusion.3), kind=kOutput, calls=%fused_computation.16 | convolution fusion | flops 4835377152 | bytes 19267584 | tf_op jit(solution)/shard_map/mgld,ldf->mglf/dot_general | solution.py:9
  356.7 9.5 %convert_bitcast_fusion = bf16[24,64,1,4096]{3,1,0,2:T(8,128)(2,1)} fusion(bf16[1,384,4096]{2,1,0:T(8,128)(2,1)S(1)} %copy-done, bf16[24,64,384]{2,0,1:T(8,128)(2,1)S(1)} %fusion.11), kind=kOutput, calls=%fused_computation.1 | convolution fusion | flops 4838129664 | bytes 16908288 | tf_op jit(solution)/shard_map/mglf,lfd->mgld/dot_general | solution.py:11
  366.3 112.8 %reduce-scatter.2.cloned.1.call-done = bf16[6,64,4096]{2,1,0:T(8,128)(2,1)} async-done(((bf16[24,64,4096]{2,1,0:T(8,128)(2,1)}), bf16[6,64,4096]{2,1,0:T(8,128)(2,1)}) %reduce-scatter.2.cloned.1.call-update) | async-done | bytes 3145744 | tf_op jit(solution)/shard_map/reduce_scatter | solution.py:57
  479.1 5.6 copy.31
  484.7 10.9 %all-to-all-start.1 = ((bf16[6,64,4096]{2,0,1:T(8,128)(2,1)}), bf16[6,64,4096]{2,0,1:T(8,128)(2,1)}, u32[]{:S(2)}, u32[]{:S(2)}) async-start(bf16[6,64,4096]{2,0,1:T(8,128)(2,1)} %copy.31), calls=%async_computation.2 | async-start | bytes 8388608 | tf_op jit(solution)/shard_map/all_to_all | solution.py:65
  495.6 0.1 reshape.110
  495.8 0.1 copy.34
  495.8 95.9 %all-to-all-done.1 = bf16[6,64,4096]{2,0,1:T(8,128)(2,1)} async-done(((bf16[6,64,4096]{2,0,1:T(8,128)(2,1)}), bf16[6,64,4096]{2,0,1:T(8,128)(2,1)}, u32[]{:S(2)}, u32[]{:S(2)}) %all-to-all-start.1) | async-done | bytes 3145760 | tf_op jit(solution)/shard_map/all_to_all | solution.py:65
  591.7 5.6 copy.32
  597.3 5.5 gather_fusion
  602.8 2.7 multiply_reduce_fusion
  (17 shorter events, 0.1 us)
Async XLA Ops:
  6.5 350.2 %copy-start = (bf16[1,384,4096]{2,1,0:T(8,128)(2,1)S(1)}, bf16[1,384,4096]{2,1,0:T(8,128)(2,1)}, u32[]{:S(2)}) copy-start(bf16[1,384,4096]{2,1,0:T(8,128)(2,1)} %param.11) | copy-start | bytes 9437188
  6.5 472.6 %reduce-scatter.2.cloned.1.call-start = ((), (), s32[]{:S(2)}) async-start(), calls=%async_computation.3 | async-start | bytes 15728640 | tf_op jit(solution)/shard_map/reduce_scatter | solution.py:57
  54.2 288.1 %copy-start.2 = (bf16[1,4096,384]{2,1,0:T(8,128)(2,1)S(1)}, bf16[1,4096,384]{2,1,0:T(8,128)(2,1)}, u32[]{:S(2)}) copy-start(bf16[1,4096,384]{2,1,0:T(8,128)(2,1)} %param.9) | copy-start | bytes 9437188
  342.2 6.9 %copy-start.3 = (bf16[1,4096,384]{2,1,0:T(8,128)(2,1)S(1)}, bf16[1,4096,384]{2,1,0:T(8,128)(2,1)}, u32[]{:S(2)}) copy-start(bf16[1,4096,384]{2,1,0:T(8,128)(2,1)} %param.10) | copy-start | bytes 9437188
  484.7 11.0 %copy-start.1 = (f32[16,8]{0,1:T(8,128)S(1)}, f32[16,8]{0,1:T(8,128)}, u32[]{:S(2)}) copy-start(f32[16,8]{0,1:T(8,128)} %param.8) | copy-start | bytes 1540
  484.7 107.0 %all-to-all-start.1 = ((bf16[6,64,4096]{2,0,1:T(8,128)(2,1)}), bf16[6,64,4096]{2,0,1:T(8,128)(2,1)}, u32[]{:S(2)}, u32[]{:S(2)}) async-start(bf16[6,64,4096]{2,0,1:T(8,128)(2,1)} %copy.31), calls=%async_computation.2 | async-start | bytes 8388608 | tf_op jit(solution)/shard_map/all_to_all | solution.py:65
Sparse Core Ops, SparseCore 0:
  366.4 112.6 reduce-scatter.1
where the time goes:
time: 613 us; the launch traced here: 612 us
  blocking collectives  313 us (51%)
  waiting for transfers between devices  209 us (34%)
  local copies, waits for them, and re-layouts  34.7 us (6%)
  matrix products  27.7 us (5%)
  between operations  13.5 us (2%)
  starting transfers between devices  10.9 us (2%)
    all_to_all x1, blocking collectives, local(): lax.all_to_all(copies.reshape(n_rep * capacity, experts, width), 'exp', s...  288 us
    reduce_scatter x1, waiting for transfers between devices, local(): lax.psum_scatter(expert_rows(row_block, w_gate, w_up, w_down).reshape(lax...  113 us
    all_to_all x1, waiting for transfers between devices, local(): lax.all_to_all(summed, 'exp', split_axis=1, concat_axis=1, tiled=True)  95.9 us
    reshape x1, local copies, waits for them, and re-layouts, local(): copies.reshape(n_rep * capacity, experts, width)  16.8 us
    all_gather x1, blocking collectives, local(): lax.all_gather(hidden_states, 'rep', axis=0, tiled=True)  13 us
    all_gather x1, blocking collectives, local(): lax.all_gather(select, 'rep', axis=0, tiled=True)  12.4 us
  transfers between devices with their start and end apart: 2, of which 2 were waited for; matrix products, arithmetic and copies ran while one was open for 0% of the time, Pallas kernels for 0%

commit v1 on v0

v1 whole, which is shorter than its diff:
```python
import functools

import jax
import jax.numpy as jnp
from jax import lax
from jax.experimental import pallas as pl
from jax.experimental.pallas import tpu as pltpu
from jax.sharding import PartitionSpec as P

MESH = pl.DeviceIdType.MESH
BF = jnp.bfloat16
F32 = jnp.float32

NZ, NX, NY, NC = 8, 4, 4, 2
CHUNKS = 4
NSEM = 64


def kernel(tok_ref, meta_ref, hot_ref, wg_hbm, wu_hbm, wd_hbm, out_ref,
           zt, mt, xs, xc_buf, xh, wgu, wd, acc, act, ry, hc, rx, rh, rr, tk, zr,
           sel, mcomb, send_sem, recv_sem, load_sem):
    y = lax.axis_index("rep")
    e = lax.axis_index("exp")
    z = e // 8
    xcore = lax.rem(e, 8)
    x = xcore // 2
    c = lax.rem(e, 2)
    width = tok_ref.shape[1]
    W = width // CHUNKS
    NT = W // 256

    def add(v, k, n):
        return lax.rem(v + (k + n), n)

    def dev_z(k):
        return {"rep": y, "exp": add(z, k, NZ) * 8 + xcore}

    def dev_x(k):
        return {"rep": y, "exp": z * 8 + add(x, k, NX) * 2 + c}

    def dev_y(k):
        return {"rep": add(y, k, NY), "exp": e}

    def dev_xc(k):
        return {"rep": y, "exp": z * 8 + lax.rem(xcore + k, 8)}

    dev_sib = {"rep": y, "exp": z * 8 + x * 2 + (1 - c)}

    loads = [
        pltpu.make_async_copy(wg_hbm.at[0], wgu.at[:, pl.ds(0, 384)], load_sem.at[0]),
        pltpu.make_async_copy(wu_hbm.at[0], wgu.at[:, pl.ds(384, 384)], load_sem.at[1]),
        pltpu.make_async_copy(wd_hbm.at[0], wd, load_sem.at[2]),
    ]
    for cp in loads:
        cp.start()

    barrier = pltpu.get_barrier_semaphore()
    partners = [dev_z(1), dev_z(-1), dev_y(1), dev_y(-1)] + [dev_xc(k) for k in range(1, 8)]
    for p in partners:
        pl.semaphore_signal(barrier, inc=1, device_id=p, device_id_type=MESH)

    for j in range(CHUNKS):
        zt[j, z] = tok_ref[:, pl.ds(j * W, W)]
    mt[z] = meta_ref[...]

    pl.semaphore_wait(barrier, len(partners))

    count = [0]
    pending = []
    copies = {}

    def send(key, src, dst, dev):
        i = count[0]
        count[0] += 1
        cp = pltpu.make_async_remote_copy(
            src_ref=src, dst_ref=dst, send_sem=send_sem.at[i], recv_sem=recv_sem.at[i],
            device_id=dev, device_id_type=MESH)
        cp.start()
        copies[key] = cp
        pending.append(key)

    def got(key):
        copies[key].wait_recv()

    def sent(match):
        for key in list(pending):
            if match(key):
                copies[key].wait_send()
                pending.remove(key)

    def hops(j):
        return (4, 3) if j % 2 == 0 else (3, 4)

    def zg_start(tag, at, j, s):
        plus, minus = hops(j)
        if s <= plus:
            slot = add(z, -(s - 1), NZ)
            send((tag, j, "p", s), at(slot), at(slot), dev_z(1))
        if s <= minus:
            slot = add(z, s - 1, NZ)
            send((tag, j, "m", s), at(slot), at(slot), dev_z(-1))

    def zg_wait(tag, j, s):
        plus, minus = hops(j)
        if s <= plus:
            got((tag, j, "p", s))
        if s <= minus:
            got((tag, j, "m", s))

    def g4_first(tag, j, at, me, dev):
        send((tag, j, "p1"), at(me, None), at(me, None), dev(1))
        send((tag, j, "m1"), at(me, None), at(me, None), dev(-1))

    def g4_second(tag, j, at, me, dev):
        left, right = add(me, -1, 4), add(me, 1, 4)
        got((tag, j, "p1"))
        send((tag, j, "p2"), at(left, 0), at(left, 0), dev(1))
        got((tag, j, "m1"))
        send((tag, j, "m2"), at(right, 1), at(right, 1), dev(-1))

    def g4_done(tag, j):
        got((tag, j, "p2"))
        got((tag, j, "m2"))

    def r4_first(tag, j, at, slot, me, dev):
        left, right, far = add(me, -1, 4), add(me, 1, 4), add(me, 2, 4)
        send((tag, j, 0), at(far, 0), slot(0), dev(1))
        send((tag, j, 2), at(far, 1), slot(2), dev(-1))
        send((tag, j, 1), at(right, 1), slot(1), dev(1))
        send((tag, j, 3), at(left, 0), slot(3), dev(-1))

    def summed(dst, *parts):
        total = parts[0][...].astype(F32)
        for part in parts[1:]:
            total = total + part[...].astype(F32)
        dst[...] = total.astype(BF)

    def tiles(dst, *parts):
        @pl.loop(0, NT)
        def _(n):
            cols = pl.ds(pl.multiple_of(n * 256, 256), 256)
            lead = (slice(None),) * (len(dst.shape) - 1)
            summed(dst.at[lead + (cols,)], *[p.at[lead + (cols,)] for p in parts])

    def r4_second(tag, j, at, slot, me, dev):
        left, right = add(me, -1, 4), add(me, 1, 4)
        got((tag, j, 0))
        tiles(at(right, 0), at(right, 0), slot(0))
        send((tag, j, 4), at(right, 0), slot(4), dev(1))
        got((tag, j, 2))
        tiles(at(left, 1), at(left, 1), slot(2))
        send((tag, j, 5), at(left, 1), slot(5), dev(-1))

    def r4_done(tag, j, at, slot, me):
        for k in (1, 3, 4, 5):
            got((tag, j, k))
        tiles(at(me, 0), at(me, 0), slot(3), slot(4))
        tiles(at(me, 1), at(me, 1), slot(1), slot(5))

    def cold_at(j):
        def at(i, half):
            return xc_buf.at[j, i] if half is None else xc_buf.at[j, i, pl.ds(4 * half, 4)]
        return at

    def hoty_at(j):
        def at(i, half):
            return xh.at[j, c, x, i] if half is None else xh.at[j, c, x, i, half]
        return at

    def hotx_at(j):
        def at(i, half):
            return xh.at[j, c, i] if half is None else xh.at[j, c, i, pl.ds(2 * half, 2)]
        return at

    def meta_done():
        both = mt[0]
        for k in range(1, NZ):
            both = both + mt[k]
        codes = both[0:8].astype(jnp.int32) - 1
        weights = both[8:16]
        row = lax.broadcasted_iota(jnp.int32, (128, 128), 0)
        want = ((row >> 1) & 7) * 512 + (z * 8 + (row >> 4)) * 8 + (row & 1)
        pick = jnp.zeros((128, 128), F32)
        comb = jnp.zeros((128, 128), F32)
        for k in range(8):
            hit = codes[k:k + 1, :] == want
            pick = pick + jnp.where(hit, 1.0, 0.0)
            comb = comb + jnp.where(hit, weights[k:k + 1, :], 0.0)
        sel[0:128, :] = pick.astype(BF)
        comb = comb.T
        high = comb.astype(BF)
        mcomb[0] = high
        mcomb[1] = (comb - high.astype(F32)).astype(BF)
        want = (row >> 2) * 512 + (row & 3) + 2
        masked = (codes >> 9) * 512 + (codes & 7)
        pick = jnp.zeros((128, 128), F32)
        comb = jnp.zeros((128, 128), F32)
        for k in range(8):
            hit = masked[k:k + 1, :] == want
            pick = pick + jnp.where(hit, 1.0, 0.0)
            comb = comb + jnp.where(hit, weights[k:k + 1, :], 0.0)
        sel[128:160, :] = pick[0:32, :].astype(BF)
        comb = comb.T
        high = comb.astype(BF)
        mcomb[2] = high
        mcomb[3] = (comb - high.astype(F32)).astype(BF)

    def d_zstart(j):
        zg_start("z", lambda s: zt.at[j, s], j, 1)
        if j == 0:
            zg_start("meta", lambda s: mt.at[s], 0, 1)

    def d_zstep(s, j):
        if j == 0:
            zg_wait("meta", 0, s - 1)
            zg_start("meta", lambda i: mt.at[i], 0, s)
        zg_wait("z", j, s - 1)
        zg_start("z", lambda i: zt.at[j, i], j, s)

    def d_select(j):
        if j == 0:
            zg_wait("meta", 0, 4)
            meta_done()
        zg_wait("z", j, 4)

        @pl.loop(0, NT)
        def _(n):
            cols = pl.ds(pl.multiple_of(n * 256, 256), 256)
            rows = jnp.dot(sel[...], zt[j, :, :, cols].reshape(128, 256), preferred_element_type=F32)
            xs[j, :, :, cols] = rows.astype(BF).reshape(10, 16, 256)

        for k in range(1, 8):
            send(("x", j, k), xs.at[j, lax.rem(xcore + k, 8)], xc_buf.at[j, y, xcore], dev_xc(k))
        xh[j, c, x, y] = xs[j, 8:10]
        g4_first("hy", j, hoty_at(j), y, dev_y)
        xc_buf[j, y, xcore] = xs[j, xcore]

    def d_hoty2(j):
        g4_second("hy", j, hoty_at(j), y, dev_y)

    def d_coldy1(j):
        for k in range(1, 8):
            got(("x", j, k))
        g4_first("cy", j, cold_at(j), y, dev_y)

    def d_hotx1(j):
        g4_done("hy", j)
        g4_first("hx", j, hotx_at(j), x, dev_x)

    def d_coldy2(j):
        g4_second("cy", j, cold_at(j), y, dev_y)

    def d_hotx2(j):
        g4_second("hx", j, hotx_at(j), x, dev_x)

    def gate_up(j, block, at, shape, first):
        @pl.loop(0, 3)
        def _(n):
            cols = pl.ds(pl.multiple_of(n * 256, 256), 256)
            part = jnp.dot(at[...].reshape(512, W), wgu[pl.ds(j * W, W), cols],
                           preferred_element_type=F32)
            if first:
                acc[block, :, cols] = part
            else:
                acc[block, :, cols] += part

    def d_coldmm(j):
        g4_done("cy", j)
        if j == 0:
            loads[0].wait()
            loads[1].wait()
        gate_up(j, 0, xc_buf.at[j], (4, 8, 16), j == 0)

    def d_core(j):
        g4_done("hx", j)
        send(("core", j), xh.at[j, c], xh.at[j, c], dev_sib)

    def d_hotmm(j):
        got(("core", j))
        gate_up(j, 1, xh.at[j, 0], (4, 4, 2, 16), j == 0)
        gate_up(j, 2, xh.at[j, 1], (4, 4, 2, 16), j == 0)

    def activate(block, masked):
        @pl.loop(0, 8)
        def _(i):
            rows = pl.ds(pl.multiple_of(i * 64, 64), 64)
            gate = acc[block, rows, 0:384]
            up = acc[block, rows, 384:768]
            value = gate / (1.0 + jnp.exp(-gate)) * up
            if masked:
                value = jnp.where(hot_ref[0:1, 0:1] > 0.5, value, 0.0)
            act[block, rows, :] = value.astype(BF)

    def down(j, block, at, shape):
        @pl.loop(0, NT)
        def _(n):
            cols = pl.ds(pl.multiple_of(n * 256, 256), 256)
            wcols = pl.ds(pl.multiple_of(j * W + n * 256, 256), 256)
            part = jnp.dot(act[block], wd[:, wcols], preferred_element_type=F32)
            at[(slice(None),) * len(shape) + (cols,)] = part.astype(BF).reshape(shape + (256,))

    def silu_cold():
        loads[2].wait()
        activate(0, False)

    def silu_hot():
        activate(1, True)
        activate(2, True)

    def ry_at(j):
        return lambda k: ry.at[j, k]

    def rx_at(j):
        return lambda k: rx.at[j, k]

    def rh_at(j):
        return lambda k: rh.at[j, k]

    def e_down(j):
        sent(lambda key: key[0] == "cy" and key[1] == j)
        down(j, 0, xc_buf.at[j], (4, 8, 16))
        r4_first("ry", j, cold_at(j), ry_at(j), y, dev_y)

    def e_second(j):
        r4_second("ry", j, cold_at(j), ry_at(j), y, dev_y)

    def e_return(j):
        r4_done("ry", j, cold_at(j), ry_at(j), y)
        for k in range(1, 8):
            send(("back", j, k), xc_buf.at[j, y, lax.rem(xcore + k, 8)], rr.at[j, xcore], dev_xc(k))
        rr[j, xcore] = xc_buf[j, y, xcore]

    def f_down(j):
        sent(lambda key: key[0] in ("hy", "hx", "core") and key[1] == j)
        down(j, 1, xh.at[j, 0], (4, 4, 2, 16))
        down(j, 2, xh.at[j, 1], (4, 4, 2, 16))
        send(("hcore", j), xh.at[j, 1 - c], hc.at[j], dev_sib)

    def f_x1(j):
        got(("hcore", j))
        for i in range(4):
            tiles(xh.at[j, c, i], xh.at[j, c, i], hc.at[j, i])
        r4_first("rx", j, hotx_at(j), rx_at(j), x, dev_x)

    def f_x2(j):
        r4_second("rx", j, hotx_at(j), rx_at(j), x, dev_x)

    def f_y1(j):
        r4_done("rx", j, hotx_at(j), rx_at(j), x)
        r4_first("rh", j, hoty_at(j), rh_at(j), y, dev_y)

    def f_y2(j):
        r4_second("rh", j, hoty_at(j), rh_at(j), y, dev_y)

    def f_done(j):
        r4_done("rh", j, hoty_at(j), rh_at(j), y)

    def zsend(j, s):
        plus, minus = hops(j)
        if s <= plus:
            send(("rz", j, "p", s), tk.at[j, add(z, plus - s + 1, NZ)], zr.at[j, s - 1], dev_z(1))
        if s <= minus:
            send(("rz", j, "m", s), tk.at[j, add(z, -(minus - s + 1), NZ)], zr.at[j, plus + s - 1], dev_z(-1))

    def g_combine(j):
        for k in range(1, 8):
            got(("back", j, k))

        @pl.loop(0, NT)
        def _(n):
            cols = pl.ds(pl.multiple_of(n * 256, 256), 256)
            cold = rr[j, :, :, cols].reshape(128, 256)
            hot = xh[j, c, x, y, :, :, cols].reshape(32, 256)
            total = jnp.dot(mcomb[0], cold, preferred_element_type=F32)
            total += jnp.dot(mcomb[1], cold, preferred_element_type=F32)
            total += jnp.dot(mcomb[2][:, 0:32], hot, preferred_element_type=F32)
            total += jnp.dot(mcomb[3][:, 0:32], hot, preferred_element_type=F32)
            tk[j, :, :, cols] = total.astype(BF).reshape(8, 16, 256)

        zsend(j, 1)

    def g_step(s, j):
        plus, minus = hops(j)
        if s - 1 <= plus:
            got(("rz", j, "p", s - 1))
            if s <= plus:
                b = add(z, plus - s + 1, NZ)
                summed(tk.at[j, b], tk.at[j, b], zr.at[j, s - 2])
        if s - 1 <= minus:
            got(("rz", j, "m", s - 1))
            if s <= minus:
                b = add(z, -(minus - s + 1), NZ)
                summed(tk.at[j, b], tk.at[j, b], zr.at[j, plus + s - 2])
        if s <= 4:
            zsend(j, s)
        else:
            summed(out_ref.at[:, pl.ds(j * W, W)], tk.at[j, z], zr.at[j, plus - 1], zr.at[j, 6])

    dispatch = [d_zstart] + [functools.partial(d_zstep, s) for s in (2, 3, 4)] + [
        d_select, d_hoty2, d_coldy1, d_hotx1, d_coldy2, d_hotx2, d_coldmm, d_core, d_hotmm]
    order = sorted((s + 2 * j, s, j) for s in range(len(dispatch)) for j in range(CHUNKS))
    done_cold = 0
    queue = []
    for _, s, j in order:
        dispatch[s](j)
        if dispatch[s] is d_coldmm:
            done_cold += 1
            if done_cold == CHUNKS:
                silu_cold()
                for i in range(CHUNKS):
                    e_down(i)
    silu_hot()
    hot = [f_down, f_x1, f_x2, f_y1, f_y2, f_done]
    cold = [None, e_second, e_return]
    last = [g_combine] + [functools.partial(g_step, s) for s in (2, 3, 4, 5)]
    stages = [(f_down,), (e_second, f_x1), (f_x2, e_return), (f_y1,), (f_y2,), (f_done, last[0])] + [(g,) for g in last[1:]]
    order = sorted((s + 2 * j, s, j) for s in range(len(stages)) for j in range(CHUNKS))
    for _, s, j in order:
        for f in stages[s]:
            f(j)
    sent(lambda key: True)


def local(hidden_states, expert_ids, route_weights, w_gate, w_up, w_down):
    rows, width = hidden_states.shape
    topk = expert_ids.shape[1]
    W = width // CHUNKS
    e = lax.axis_index("exp")
    z = e // 8
    flat = expert_ids.reshape(-1)
    token = jnp.arange(rows * topk, dtype=jnp.int32) // topk
    earlier = (flat[:, None] == flat[None, :]) & (token[None, :] < token[:, None])
    rank = jnp.sum(earlier.astype(jnp.int32), axis=1).reshape(rows, topk)
    hot_id = jnp.max(jnp.where(rank >= 2, expert_ids, -1))
    code = (z * 512 + expert_ids * 8 + rank + 1).astype(F32)
    norm = route_weights / jnp.sum(route_weights, axis=1, keepdims=True)
    both = jnp.concatenate([code.T, norm.T], axis=0)
    mine = jnp.arange(128, dtype=jnp.int32) // rows == z
    meta = jnp.where(mine[None, :], jnp.tile(both, (1, NZ)), 0.0)
    hot = jnp.full((8, 128), jnp.where(hot_id == e, 1.0, 0.0), F32)

    vmem = pl.BlockSpec(memory_space=pltpu.VMEM)
    hbm = pl.BlockSpec(memory_space=pl.ANY)
    C = CHUNKS
    scratch = [
        pltpu.VMEM((C, 8, 16, W), BF),
        pltpu.VMEM((8, 16, 128), F32),
        pltpu.VMEM((C, 10, 16, W), BF),
        pltpu.VMEM((C, 4, 8, 16, W), BF),
        pltpu.VMEM((C, 2, 4, 4, 2, 16, W), BF),
        pltpu.VMEM((width, 768), BF),
        pltpu.VMEM((384, width), BF),
        pltpu.VMEM((3, 512, 768), F32),
        pltpu.VMEM((3, 512, 384), BF),
        pltpu.VMEM((C, 6, 4, 16, W), BF),
        pltpu.VMEM((C, 4, 4, 2, 16, W), BF),
        pltpu.VMEM((C, 6, 2, 2, 16, W), BF),
        pltpu.VMEM((C, 6, 16, W), BF),
        pltpu.VMEM((C, 8, 16, W), BF),
        pltpu.VMEM((C, 8, 16, W), BF),
        pltpu.VMEM((C, 7, 16, W), BF),
        pltpu.VMEM((160, 128), BF),
        pltpu.VMEM((4, 128, 128), BF),
        pltpu.SemaphoreType.DMA((C * NSEM + 8,)),
        pltpu.SemaphoreType.DMA((C * NSEM + 8,)),
        pltpu.SemaphoreType.DMA((3,)),
    ]
    return pl.pallas_call(
        kernel,
        out_shape=jax.ShapeDtypeStruct((rows, width), BF),
        in_specs=[vmem, vmem, vmem, hbm, hbm, hbm],
        out_specs=vmem,
        scratch_shapes=scratch,
        compiler_params=pltpu.CompilerParams(
            collective_id=0, has_side_effects=True, vmem_limit_bytes=60 * 1024 * 1024),
    )(hidden_states, meta, hot, w_gate, w_up, w_down)


def solution(mesh):
    in_specs = (
        P(("rep", "exp"), None),
        P(("rep", "exp"), None),
        P(("rep", "exp"), None),
        P("exp", None, "rep"),
        P("exp", None, "rep"),
        P("exp", "rep", None),
    )
    out_specs = P(("rep", "exp"), None)
    return jax.shard_map(local, mesh=mesh, in_specs=in_specs, out_specs=out_specs, check_vma=False)
```

time: 613 us -> 173 us (0.28)
  blocking collectives: 313 us -> 0 us
  waiting for transfers between devices: 209 us -> 0 us
  Pallas kernels: 0 us -> 164 us
  local copies, waits for them, and re-layouts: 34.7 us -> 3.24 us
  matrix products: 27.7 us -> 0 us
  between operations: 13.5 us -> 0.67 us
  starting transfers between devices: 10.9 us -> 0 us
    all_to_all x1 -> x0, blocking collectives: 288 us -> none  [local(): lax.all_to_all(copies.reshape(n_rep * capacity, experts, width), 'exp', s...]
    pallas_call x0 -> x1, Pallas kernels: none -> 164 us  [local(): pl.pallas_call(kernel, out_shape=jax.ShapeDtypeStruct((rows, width), BF),...]
    reduce_scatter x1 -> x0, waiting for transfers between devices: 113 us -> none  [local(): lax.psum_scatter(expert_rows(row_block, w_gate, w_up, w_down).reshape(lax...]
    all_to_all x1 -> x0, waiting for transfers between devices: 95.9 us -> none  [local(): lax.all_to_all(summed, 'exp', split_axis=1, concat_axis=1, tiled=True)]
    dot_general x4 -> x0, matrix products: 27.7 us -> none  [the longest x1 9.55 us: expert_rows(): jnp.einsum('mglf,lfd->mgld', active, down_w, preferred_element_type=jnp.f...]
    all_gather x2 -> x0, blocking collectives: 25.4 us -> none  [the longest x1 13 us: local(): lax.all_gather(hidden_states, 'rep', axis=0, tiled=True)]
    reshape x2, local copies, waits for them, and re-layouts: 16.9 us -> 0.15 us  [local(): rank = jnp.sum(earlier.astype(jnp.int32), axis=1).reshape(rows, topk)]
    all_to_all x1 -> x0, starting transfers between devices: 10.9 us -> none  [local(): lax.all_to_all(summed, 'exp', split_axis=1, concat_axis=1, tiled=True)]
  transfers between devices with their start and end apart: 2 -> 0, of which waited for: 2 -> 0; matrix products, arithmetic and copies ran while one was open for 0% -> 0% of each run, Pallas kernels for 0% -> 0%
where the time goes in v1:
time: 173 us; the launch traced here: 172 us
  Pallas kernels  164 us (95%)
  other arithmetic  3.55 us (2%)
  local copies, waits for them, and re-layouts  3.24 us (2%)
    pallas_call x1, Pallas kernels, local(): pl.pallas_call(kernel, out_shape=jax.ShapeDtypeStruct((rows, width), BF),...  164 us

profile of v1, /device:TPU:2, one launch (start us, length us, event | category | flops | bytes accessed | tf_op | source)
XLA Modules:
  0.0 171.9 jit_solution(12315597850903391490)
XLA Ops:
  0.0 0.7 reduce_sum.19
  0.7 0.7 divide_bitcast_fusion
  1.4 0.8 copy.22
  2.2 0.1 eq.30
  2.3 0.2 convert_reduce_fusion
  2.4 0.1 reshape.51
  2.5 0.7 select_reduce_fusion
  3.8 0.1 copy.23
  3.9 0.7 convert_bitcast_fusion
  4.6 0.6 broadcast_in_dim.26.hot_ref
  5.2 0.1 tile.10
  5.3 0.6 broadcast_select_fusion.meta_ref
  5.9 164.5 %shard_map.64 = bf16[16,4096]{1,0:T(8,128)(2,1)} custom-call(bf16[16,4096]{1,0:T(8,128)(2,1)} %tok_ref.1, f32[16,128]{1,0:T(8,128)} %broadcast_select_fusion.meta_ref, f32[8,128]{1,0:T(8,128)} %broadcast_in_dim.26.hot_ref, bf16[1,4096,384]{2,1,0:T(8,128)(2,1)} %wg_hbm.1, bf16[1,4096,384]{2,1,0:T(8,128)(2,1)} %wu_hbm.1, bf16[1,384,4096]{2,1,0:T(8,128)(2,1)} %wd_hbm.1), custom_call_target="tpu_custom_call" | custom-call | tf_op jit(solution)/shard_map/pallas_call | solution.py:468
  170.4 1.6 copy.26
  (4 shorter events, 0.0 us)

commit v2 on v1

--- a/solution.py
+++ b/solution.py
@@ -13,12 +13,32 @@
 
 NZ, NX, NY, NC = 8, 4, 4, 2
 CHUNKS = 4
-NSEM = 64
-
-
-def kernel(tok_ref, meta_ref, hot_ref, wg_hbm, wu_hbm, wd_hbm, out_ref,
+NSEM = 80
+ZLAST = (2, 3)
+
+ORDER = (
+    ("z1", 2), ("z1", 3), ("z1", 0), ("z1", 1), ("z2", 2), ("z2", 3), ("z2", 0), ("z3", 2), ("z3", 3),
+    ("z3", 0), ("z2", 1), ("z4", 2), ("z4", 3), ("z4", 0), ("sel", 3), ("sel", 0), ("hy2", 3), ("z3", 1),
+    ("sel", 2), ("hy2", 2), ("z4", 1), ("cy1", 3), ("hx1", 2), ("hy2", 0), ("hx1", 3), ("hx2", 2),
+    ("sel", 1), ("cy2", 3), ("hz1", 2), ("hx2", 3), ("hx1", 0), ("hy2", 1), ("hz1", 3), ("cy1", 0),
+    ("cy1", 2), ("hz2", 2), ("cy1", 1), ("hx1", 1), ("hz2", 3), ("hx2", 0), ("cmm", 3), ("hz3", 2),
+    ("hz3", 3), ("hx2", 1), ("core", 0), ("cy2", 2), ("hz4", 2), ("hz4", 3), ("cy2", 0), ("core", 1),
+    ("hmm", 0), ("cy2", 1), ("core", 3), ("hmm", 1), ("core", 2), ("cmm", 2), ("hmm", 3), ("cmm", 0),
+    ("cmm", 1), ("silc", 0), ("edn", 1), ("edn", 3), ("edn", 0), ("edn", 2), ("hmm", 2), ("silh", 0),
+    ("fdn", 2), ("fdn", 3), ("fdn", 0), ("fz1", 2), ("fz1", 3), ("fx1", 0), ("fdn", 1), ("fz2", 2),
+    ("fx2", 0), ("fz2", 3), ("fx1", 1), ("fz3", 2), ("e2", 2), ("fz3", 3), ("e2", 0), ("fx2", 1), ("fz4", 2),
+    ("fy1", 0), ("e2", 1), ("e2", 3), ("fz4", 3), ("ret", 0), ("fy1", 1), ("fx1", 2), ("fx1", 3), ("ret", 1),
+    ("fy2", 0), ("fx2", 2), ("fx2", 3), ("ret", 2), ("ret", 3), ("fy2", 1), ("fdone", 0), ("comb", 0),
+    ("fy1", 2), ("fy1", 3), ("fdone", 1), ("comb", 1), ("fy2", 3), ("fy2", 2), ("fdone", 2), ("comb", 2),
+    ("gz2", 1), ("gz2", 0), ("fdone", 3), ("comb", 3), ("gz2", 2), ("gz3", 0), ("gz2", 3), ("gz3", 1),
+    ("gz3", 2), ("gz3", 3), ("gz4", 1), ("gz4", 0), ("gz4", 2), ("gz4", 3), ("out", 1), ("out", 2),
+    ("out", 0), ("out", 3),
+)
+
+
+def kernel(tok_ref, ids_ref, route_ref, wg_hbm, wu_hbm, wd_hbm, out_ref,
            zt, mt, xs, xc_buf, xh, wgu, wd, acc, act, ry, hc, rx, rh, rr, tk, zr,
-           sel, mcomb, send_sem, recv_sem, load_sem):
+           zh, hot_ref, sel, mcomb, send_sem, recv_sem, load_sem):
     y = lax.axis_index("rep")
     e = lax.axis_index("exp")
     z = e // 8
@@ -28,6 +48,8 @@
     width = tok_ref.shape[1]
     W = width // CHUNKS
     NT = W // 256
+    S = W // NZ
+    zcols = pl.ds(pl.multiple_of(z * S, S), S)
 
     def add(v, k, n):
         return lax.rem(v + (k + n), n)
@@ -55,13 +77,36 @@
         cp.start()
 
     barrier = pltpu.get_barrier_semaphore()
-    partners = [dev_z(1), dev_z(-1), dev_y(1), dev_y(-1)] + [dev_xc(k) for k in range(1, 8)]
+    partners = [dev_z(k) for k in range(1, 8)] + [dev_y(1), dev_y(-1)] + [dev_xc(k) for k in range(1, 8)]
     for p in partners:
         pl.semaphore_signal(barrier, inc=1, device_id=p, device_id_type=MESH)
 
     for j in range(CHUNKS):
         zt[j, z] = tok_ref[:, pl.ds(j * W, W)]
-    mt[z] = meta_ref[...]
+
+    ids = ids_ref[...]
+    route = route_ref[...]
+    norm = route / jnp.sum(route, axis=0, keepdims=True)
+    expert = lax.broadcasted_iota(jnp.int32, (64, 16), 0)
+    named = jnp.zeros((64, 16), F32)
+    for k in range(8):
+        named = named + jnp.where(ids[k:k + 1, :] == expert, 1.0, 0.0)
+    before = (lax.broadcasted_iota(jnp.int32, (16, 16), 0) < lax.broadcasted_iota(jnp.int32, (16, 16), 1))
+    earlier = jnp.dot(named.astype(BF), jnp.where(before, 1.0, 0.0).astype(BF), preferred_element_type=F32)
+    ranks = [jnp.sum(jnp.where(ids[k:k + 1, :] == expert, earlier, 0.0), axis=0, keepdims=True)
+             for k in range(8)]
+    rank = jnp.concatenate(ranks, axis=0)
+    is_hot = jnp.where((ids == e) & (rank > 1.5), 1.0, 0.0)
+    hot_ref[...] = jnp.broadcast_to(jnp.max(jnp.max(is_hot, axis=1, keepdims=True), axis=0, keepdims=True), (8, 128))
+    high = norm.astype(BF)
+    table = jnp.concatenate([ids.astype(F32), rank, high.astype(F32), norm - high.astype(F32)], axis=0)
+    lane = lax.broadcasted_iota(jnp.int32, (16, 128), 1)
+    place = jnp.where(lane == z * 16 + lax.broadcasted_iota(jnp.int32, (16, 128), 0), 1.0, 0.0)
+    placed = jnp.dot(table.astype(BF), place.astype(BF), preferred_element_type=F32)
+    own = (lax.broadcasted_iota(jnp.int32, (8, 128), 1) >> 4) == z
+    base = (z * 512 + 1).astype(F32)
+    mt[z, 0:8, :] = jnp.where(own, placed[0:8] * 8.0 + placed[8:16] + base, 0.0)
+    mt[z, 8:16, :] = placed[16:24] + placed[24:32]
 
     pl.semaphore_wait(barrier, len(partners))
 
@@ -136,6 +181,10 @@
         dst[...] = total.astype(BF)
 
     def tiles(dst, *parts):
+        if dst.shape[-1] < 256:
+            summed(dst, *parts)
+            return
+
         @pl.loop(0, NT)
         def _(n):
             cols = pl.ds(pl.multiple_of(n * 256, 256), 256)
@@ -164,13 +213,22 @@
 
     def hoty_at(j):
         def at(i, half):
+            if j in ZLAST:
+                return xh.at[j, c, x, i, :, :, zcols] if half is None else xh.at[j, c, x, i, half, :, zcols]
             return xh.at[j, c, x, i] if half is None else xh.at[j, c, x, i, half]
         return at
 
     def hotx_at(j):
         def at(i, half):
+            if j in ZLAST:
+                if half is None:
+                    return xh.at[j, c, i, :, :, :, zcols]
+                return xh.at[j, c, i, pl.ds(2 * half, 2), :, :, zcols]
             return xh.at[j, c, i] if half is None else xh.at[j, c, i, pl.ds(2 * half, 2)]
         return at
+
+    def slice_at(j):
+        return lambda k: xh.at[j, c, :, :, :, :, pl.ds(pl.multiple_of(k * S, S), S)]
 
     def meta_done():
         both = mt[0]
@@ -208,18 +266,21 @@
     def d_zstart(j):
         zg_start("z", lambda s: zt.at[j, s], j, 1)
         if j == 0:
-            zg_start("meta", lambda s: mt.at[s], 0, 1)
+            for k in range(1, NZ):
+                send(("meta", k), mt.at[z], mt.at[z], dev_z(k))
 
     def d_zstep(s, j):
-        if j == 0:
-            zg_wait("meta", 0, s - 1)
-            zg_start("meta", lambda i: mt.at[i], 0, s)
         zg_wait("z", j, s - 1)
         zg_start("z", lambda i: zt.at[j, i], j, s)
 
+    ready = []
+    started = set()
+
     def d_select(j):
-        if j == 0:
-            zg_wait("meta", 0, 4)
+        if not ready:
+            ready.append(j)
+            for k in range(1, NZ):
+                got(("meta", k))
             meta_done()
         zg_wait("z", j, 4)
 
@@ -231,7 +292,10 @@
 
         for k in range(1, 8):
             send(("x", j, k), xs.at[j, lax.rem(xcore + k, 8)], xc_buf.at[j, y, xcore], dev_xc(k))
-        xh[j, c, x, y] = xs[j, 8:10]
+        if j in ZLAST:
+            xh[j, c, x, y, :, :, zcols] = xs[j, 8:10, :, zcols]
+        else:
+            xh[j, c, x, y] = xs[j, 8:10]
         g4_first("hy", j, hoty_at(j), y, dev_y)
         xc_buf[j, y, xcore] = xs[j, xcore]
 
@@ -253,7 +317,17 @@
     def d_hotx2(j):
         g4_second("hx", j, hotx_at(j), x, dev_x)
 
-    def gate_up(j, block, at, shape, first):
+    def d_hotz(s, j):
+        if s == 1:
+            g4_done("hx", j)
+        else:
+            zg_wait("hz", j, s - 1)
+        zg_start("hz", slice_at(j), j, s)
+
+    def gate_up(j, block, at):
+        first = block not in started
+        started.add(block)
+
         @pl.loop(0, 3)
         def _(n):
             cols = pl.ds(pl.multiple_of(n * 256, 256), 256)
@@ -264,21 +338,28 @@
             else:
                 acc[block, :, cols] += part
 
+    def weights_in():
+        if not started:
+            loads[0].wait()
+            loads[1].wait()
+
     def d_coldmm(j):
         g4_done("cy", j)
-        if j == 0:
-            loads[0].wait()
-            loads[1].wait()
-        gate_up(j, 0, xc_buf.at[j], (4, 8, 16), j == 0)
+        weights_in()
+        gate_up(j, 0, xc_buf.at[j])
 
     def d_core(j):
-        g4_done("hx", j)
+        if j in ZLAST:
+            zg_wait("hz", j, 4)
+        else:
+            g4_done("hx", j)
         send(("core", j), xh.at[j, c], xh.at[j, c], dev_sib)
 
     def d_hotmm(j):
         got(("core", j))
-        gate_up(j, 1, xh.at[j, 0], (4, 4, 2, 16), j == 0)
-        gate_up(j, 2, xh.at[j, 1], (4, 4, 2, 16), j == 0)
+        weights_in()
+        gate_up(j, 1, xh.at[j, 0])
+        gate_up(j, 2, xh.at[j, 1])
 
     def activate(block, masked):
         @pl.loop(0, 8)
@@ -299,11 +380,11 @@
             part = jnp.dot(act[block], wd[:, wcols], preferred_element_type=F32)
             at[(slice(None),) * len(shape) + (cols,)] = part.astype(BF).reshape(shape + (256,))
 
-    def silu_cold():
+    def silu_cold(j):
         loads[2].wait()
         activate(0, False)
 
-    def silu_hot():
+    def silu_hot(j):
         activate(1, True)
         activate(2, True)
 
@@ -311,9 +392,13 @@
         return lambda k: ry.at[j, k]
 
     def rx_at(j):
+        if j in ZLAST:
+            return lambda k: rx.at[j, k, :, :, :, pl.ds(0, S)]
         return lambda k: rx.at[j, k]
 
     def rh_at(j):
+        if j in ZLAST:
+            return lambda k: rh.at[j, k, :, pl.ds(0, S)]
         return lambda k: rh.at[j, k]
 
     def e_down(j):
@@ -331,15 +416,53 @@
         rr[j, xcore] = xc_buf[j, y, xcore]
 
     def f_down(j):
-        sent(lambda key: key[0] in ("hy", "hx", "core") and key[1] == j)
+        sent(lambda key: key[0] in ("hy", "hx", "hz", "core") and key[1] == j)
         down(j, 1, xh.at[j, 0], (4, 4, 2, 16))
         down(j, 2, xh.at[j, 1], (4, 4, 2, 16))
         send(("hcore", j), xh.at[j, 1 - c], hc.at[j], dev_sib)
 
-    def f_x1(j):
+    def core_sum(j):
         got(("hcore", j))
         for i in range(4):
             tiles(xh.at[j, c, i], xh.at[j, c, i], hc.at[j, i])
+
+    def ring_send(tag, j, s, block, slot):
+        plus, minus = hops(j)
+        if s <= plus:
+            send((tag, j, "p", s), block(add(z, plus - s + 1, NZ)), slot(s - 1), dev_z(1))
+        if s <= minus:
+            send((tag, j, "m", s), block(add(z, -(minus - s + 1), NZ)), slot(plus + s - 1), dev_z(-1))
+
+    def ring_sum(tag, j, s, block, slot):
+        plus, minus = hops(j)
+        if s - 1 <= plus:
+            got((tag, j, "p", s - 1))
+            if s <= plus:
+                b = add(z, plus - s + 1, NZ)
+                summed(block(b), block(b), slot(s - 2))
+        if s - 1 <= minus:
+            got((tag, j, "m", s - 1))
+            if s <= minus:
+                b = add(z, -(minus - s + 1), NZ)
+                summed(block(b), block(b), slot(plus + s - 2))
+
+    def zh_at(j):
+        return lambda k: zh.at[ZLAST.index(j), k]
+
+    def f_z(s, j):
+        if s == 1:
+            core_sum(j)
+        else:
+            ring_sum("fz", j, s, slice_at(j), zh_at(j))
+        ring_send("fz", j, s, slice_at(j), zh_at(j))
+
+    def f_x1(j):
+        if j in ZLAST:
+            ring_sum("fz", j, 5, slice_at(j), zh_at(j))
+            mine = slice_at(j)(z)
+            summed(mine, mine, zh_at(j)(hops(j)[0] - 1), zh_at(j)(6))
+        else:
+            core_sum(j)
         r4_first("rx", j, hotx_at(j), rx_at(j), x, dev_x)
 
     def f_x2(j):
@@ -355,12 +478,11 @@
     def f_done(j):
         r4_done("rh", j, hoty_at(j), rh_at(j), y)
 
-    def zsend(j, s):
-        plus, minus = hops(j)
-        if s <= plus:
-            send(("rz", j, "p", s), tk.at[j, add(z, plus - s + 1, NZ)], zr.at[j, s - 1], dev_z(1))
-        if s <= minus:
-            send(("rz", j, "m", s), tk.at[j, add(z, -(minus - s + 1), NZ)], zr.at[j, plus + s - 1], dev_z(-1))
+    def tk_at(j):
+        return lambda k: tk.at[j, k]
+
+    def zr_at(j):
+        return lambda k: zr.at[j, k]
 
     def g_combine(j):
         for k in range(1, 8):
@@ -370,75 +492,52 @@
         def _(n):
             cols = pl.ds(pl.multiple_of(n * 256, 256), 256)
             cold = rr[j, :, :, cols].reshape(128, 256)
-            hot = xh[j, c, x, y, :, :, cols].reshape(32, 256)
             total = jnp.dot(mcomb[0], cold, preferred_element_type=F32)
             total += jnp.dot(mcomb[1], cold, preferred_element_type=F32)
-            total += jnp.dot(mcomb[2][:, 0:32], hot, preferred_element_type=F32)
-            total += jnp.dot(mcomb[3][:, 0:32], hot, preferred_element_type=F32)
+            if j not in ZLAST:
+                total += hot_part(xh[j, c, x, y, :, :, cols].reshape(32, 256))
             tk[j, :, :, cols] = total.astype(BF).reshape(8, 16, 256)
 
-        zsend(j, 1)
+        if j in ZLAST:
+            cold = rr[j, :, :, zcols].reshape(128, S)
+            total = jnp.dot(mcomb[0], cold, preferred_element_type=F32)
+            total += jnp.dot(mcomb[1], cold, preferred_element_type=F32)
+            total += hot_part(xh[j, c, x, y, :, :, zcols].reshape(32, S))
+            tk[j, :, :, zcols] = total.astype(BF).reshape(8, 16, S)
+        ring_send("rz", j, 1, tk_at(j), zr_at(j))
+
+    def hot_part(rows):
+        total = jnp.dot(mcomb[2][:, 0:32], rows, preferred_element_type=F32)
+        return total + jnp.dot(mcomb[3][:, 0:32], rows, preferred_element_type=F32)
 
     def g_step(s, j):
-        plus, minus = hops(j)
-        if s - 1 <= plus:
-            got(("rz", j, "p", s - 1))
-            if s <= plus:
-                b = add(z, plus - s + 1, NZ)
-                summed(tk.at[j, b], tk.at[j, b], zr.at[j, s - 2])
-        if s - 1 <= minus:
-            got(("rz", j, "m", s - 1))
-            if s <= minus:
-                b = add(z, -(minus - s + 1), NZ)
-                summed(tk.at[j, b], tk.at[j, b], zr.at[j, plus + s - 2])
-        if s <= 4:
-            zsend(j, s)
-        else:
-            summed(out_ref.at[:, pl.ds(j * W, W)], tk.at[j, z], zr.at[j, plus - 1], zr.at[j, 6])
-
-    dispatch = [d_zstart] + [functools.partial(d_zstep, s) for s in (2, 3, 4)] + [
-        d_select, d_hoty2, d_coldy1, d_hotx1, d_coldy2, d_hotx2, d_coldmm, d_core, d_hotmm]
-    order = sorted((s + 2 * j, s, j) for s in range(len(dispatch)) for j in range(CHUNKS))
-    done_cold = 0
-    queue = []
-    for _, s, j in order:
-        dispatch[s](j)
-        if dispatch[s] is d_coldmm:
-            done_cold += 1
-            if done_cold == CHUNKS:
-                silu_cold()
-                for i in range(CHUNKS):
-                    e_down(i)
-    silu_hot()
-    hot = [f_down, f_x1, f_x2, f_y1, f_y2, f_done]
-    cold = [None, e_second, e_return]
-    last = [g_combine] + [functools.partial(g_step, s) for s in (2, 3, 4, 5)]
-    stages = [(f_down,), (e_second, f_x1), (f_x2, e_return), (f_y1,), (f_y2,), (f_done, last[0])] + [(g,) for g in last[1:]]
-    order = sorted((s + 2 * j, s, j) for s in range(len(stages)) for j in range(CHUNKS))
-    for _, s, j in order:
-        for f in stages[s]:
-            f(j)
+        ring_sum("rz", j, s, tk_at(j), zr_at(j))
+        ring_send("rz", j, s, tk_at(j), zr_at(j))
+
+    def g_out(j):
+        ring_sum("rz", j, 5, tk_at(j), zr_at(j))
+        summed(out_ref.at[:, pl.ds(j * W, W)], tk.at[j, z], zr.at[j, hops(j)[0] - 1], zr.at[j, 6])
+
+    def stepped(f):
+        return [functools.partial(f, s) for s in range(1, 5)]
+
+    steps = {
+        "z1": d_zstart, "sel": d_select, "hy2": d_hoty2, "hx1": d_hotx1, "hx2": d_hotx2, "core": d_core,
+        "cy1": d_coldy1, "cy2": d_coldy2, "cmm": d_coldmm, "hmm": d_hotmm, "silc": silu_cold,
+        "silh": silu_hot, "edn": e_down, "e2": e_second, "ret": e_return, "fdn": f_down, "fx1": f_x1,
+        "fx2": f_x2, "fy1": f_y1, "fy2": f_y2, "fdone": f_done, "comb": g_combine, "out": g_out,
+    }
+    for name, f in (("z", d_zstep), ("hz", d_hotz), ("fz", f_z), ("gz", g_step)):
+        for s, g in enumerate(stepped(f), 1):
+            steps.setdefault(name + str(s), g)
+    for name, j in ORDER:
+        steps[name](j)
     sent(lambda key: True)
 
 
 def local(hidden_states, expert_ids, route_weights, w_gate, w_up, w_down):
     rows, width = hidden_states.shape
-    topk = expert_ids.shape[1]
     W = width // CHUNKS
-    e = lax.axis_index("exp")
-    z = e // 8
-    flat = expert_ids.reshape(-1)
-    token = jnp.arange(rows * topk, dtype=jnp.int32) // topk
-    earlier = (flat[:, None] == flat[None, :]) & (token[None, :] < token[:, None])
-    rank = jnp.sum(earlier.astype(jnp.int32), axis=1).reshape(rows, topk)
-    hot_id = jnp.max(jnp.where(rank >= 2, expert_ids, -1))
-    code = (z * 512 + expert_ids * 8 + rank + 1).astype(F32)
-    norm = route_weights / jnp.sum(route_weights, axis=1, keepdims=True)
-    both = jnp.concatenate([code.T, norm.T], axis=0)
-    mine = jnp.arange(128, dtype=jnp.int32) // rows == z
-    meta = jnp.where(mine[None, :], jnp.tile(both, (1, NZ)), 0.0)
-    hot = jnp.full((8, 128), jnp.where(hot_id == e, 1.0, 0.0), F32)
-
     vmem = pl.BlockSpec(memory_space=pltpu.VMEM)
     hbm = pl.BlockSpec(memory_space=pl.ANY)
     C = CHUNKS
@@ -459,6 +558,8 @@
         pltpu.VMEM((C, 8, 16, W), BF),
         pltpu.VMEM((C, 8, 16, W), BF),
         pltpu.VMEM((C, 7, 16, W), BF),
+        pltpu.VMEM((len(ZLAST), 7, 4, 4, 2, 16, W // NZ), BF),
+        pltpu.VMEM((8, 128), F32),
         pltpu.VMEM((160, 128), BF),
         pltpu.VMEM((4, 128, 128), BF),
         pltpu.SemaphoreType.DMA((C * NSEM + 8,)),
@@ -473,7 +574,7 @@
         scratch_shapes=scratch,
         compiler_params=pltpu.CompilerParams(
             collective_id=0, has_side_effects=True, vmem_limit_bytes=60 * 1024 * 1024),
-    )(hidden_states, meta, hot, w_gate, w_up, w_down)
+    )(hidden_states, expert_ids.T, route_weights.T, w_gate, w_up, w_down)
 
 
 def solution(mesh):

time: 173 us -> 154 us (0.89)
  Pallas kernels: 164 us -> 152 us
  other arithmetic: 3.55 us -> 0 us
    pallas_call x1, Pallas kernels: 164 us -> 152 us  [local(): pl.pallas_call(kernel, out_shape=jax.ShapeDtypeStruct((rows, width), BF),...]
where the time goes in v2:
time: 154 us; the launch traced here: 153 us
  Pallas kernels  152 us (99%)
  local copies, waits for them, and re-layouts  1.57 us (1%)
    pallas_call x1, Pallas kernels, local(): pl.pallas_call(kernel, out_shape=jax.ShapeDtypeStruct((rows, width), BF),...  152 us

profile of v2, /device:TPU:2, one launch (start us, length us, event | category | flops | bytes accessed | tf_op | source)
XLA Modules:
  0.0 153.5 jit_solution(17212362921099434680)
XLA Ops:
  0.0 151.9 %shard_map.64 = bf16[16,4096]{1,0:T(8,128)(2,1)} custom-call(bf16[16,4096]{1,0:T(8,128)(2,1)} %tok_ref.1, s32[8,16]{1,0:T(8,128)} %bitcast.2, f32[8,16]{1,0:T(8,128)} %bitcast.3, bf16[1,4096,384]{2,1,0:T(8,128)(2,1)} %wg_hbm.1, bf16[1,4096,384]{2,1,0:T(8,128)(2,1)} %wu_hbm.1, bf16[1,384,4096]{2,1,0:T(8,128)(2,1)} %wd_hbm.1), custom_call_target="tpu_custom_call" | custom-call | tf_op jit(solution)/shard_map/pallas_call | solution.py:569
  151.9 1.6 %copy.8 = bf16[16,4096]{1,0:T(8,128)(2,1)} copy(bf16[16,4096]{1,0:T(8,128)(2,1)} %shard_map.64) | data formatting | bytes 262144

commit v3 on v2

--- a/solution.py
+++ b/solution.py
@@ -12,27 +12,37 @@
 F32 = jnp.float32
 
 NZ, NX, NY, NC = 8, 4, 4, 2
-CHUNKS = 4
+WIDTHS = (1024, 1024, 512, 512, 512, 512)
+ZLAST = (0, 1)
+ZDIR = ()
+RDIR = (0, 1)
+CHUNKS = len(WIDTHS)
+OFFS = tuple(sum(WIDTHS[:i]) for i in range(CHUNKS))
 NSEM = 80
-ZLAST = (2, 3)
 
 ORDER = (
-    ("z1", 2), ("z1", 3), ("z1", 0), ("z1", 1), ("z2", 2), ("z2", 3), ("z2", 0), ("z3", 2), ("z3", 3),
-    ("z3", 0), ("z2", 1), ("z4", 2), ("z4", 3), ("z4", 0), ("sel", 3), ("sel", 0), ("hy2", 3), ("z3", 1),
-    ("sel", 2), ("hy2", 2), ("z4", 1), ("cy1", 3), ("hx1", 2), ("hy2", 0), ("hx1", 3), ("hx2", 2),
-    ("sel", 1), ("cy2", 3), ("hz1", 2), ("hx2", 3), ("hx1", 0), ("hy2", 1), ("hz1", 3), ("cy1", 0),
-    ("cy1", 2), ("hz2", 2), ("cy1", 1), ("hx1", 1), ("hz2", 3), ("hx2", 0), ("cmm", 3), ("hz3", 2),
-    ("hz3", 3), ("hx2", 1), ("core", 0), ("cy2", 2), ("hz4", 2), ("hz4", 3), ("cy2", 0), ("core", 1),
-    ("hmm", 0), ("cy2", 1), ("core", 3), ("hmm", 1), ("core", 2), ("cmm", 2), ("hmm", 3), ("cmm", 0),
-    ("cmm", 1), ("silc", 0), ("edn", 1), ("edn", 3), ("edn", 0), ("edn", 2), ("hmm", 2), ("silh", 0),
-    ("fdn", 2), ("fdn", 3), ("fdn", 0), ("fz1", 2), ("fz1", 3), ("fx1", 0), ("fdn", 1), ("fz2", 2),
-    ("fx2", 0), ("fz2", 3), ("fx1", 1), ("fz3", 2), ("e2", 2), ("fz3", 3), ("e2", 0), ("fx2", 1), ("fz4", 2),
-    ("fy1", 0), ("e2", 1), ("e2", 3), ("fz4", 3), ("ret", 0), ("fy1", 1), ("fx1", 2), ("fx1", 3), ("ret", 1),
-    ("fy2", 0), ("fx2", 2), ("fx2", 3), ("ret", 2), ("ret", 3), ("fy2", 1), ("fdone", 0), ("comb", 0),
-    ("fy1", 2), ("fy1", 3), ("fdone", 1), ("comb", 1), ("fy2", 3), ("fy2", 2), ("fdone", 2), ("comb", 2),
-    ("gz2", 1), ("gz2", 0), ("fdone", 3), ("comb", 3), ("gz2", 2), ("gz3", 0), ("gz2", 3), ("gz3", 1),
-    ("gz3", 2), ("gz3", 3), ("gz4", 1), ("gz4", 0), ("gz4", 2), ("gz4", 3), ("out", 1), ("out", 2),
-    ("out", 0), ("out", 3),
+    ("z1", 2), ("z1", 3), ("z1", 1), ("z1", 4), ("z1", 0), ("z2", 2), ("z1", 5), ("z2", 3), ("z2", 1),
+    ("z2", 4), ("z2", 0), ("z3", 2), ("z2", 5), ("z3", 3), ("z3", 1), ("z3", 4), ("z3", 0), ("z4", 2),
+    ("z4", 3), ("z4", 1), ("z3", 5), ("z4", 4), ("z4", 0), ("selh", 2), ("selc", 2), ("selh", 3),
+    ("selc", 3), ("selh", 1), ("selc", 1), ("hy2", 2), ("selh", 4), ("selh", 0), ("hy2", 3), ("cy1", 2),
+    ("z4", 5), ("hx1", 1), ("selc", 4), ("cy1", 3), ("hx1", 0), ("hx1", 2), ("selh", 5), ("hy2", 4),
+    ("hz1", 1), ("cy1", 1), ("selc", 0), ("hz1", 0), ("cy1", 4), ("hx1", 4), ("hz2", 1), ("hy2", 5),
+    ("selc", 5), ("cy2", 2), ("hx2", 2), ("hz2", 0), ("cy2", 3), ("cy2", 1), ("hx2", 4), ("hz3", 1),
+    ("hx1", 3), ("cy1", 0), ("hz3", 0), ("hx1", 5), ("cy1", 5), ("core", 4), ("core", 2), ("hz4", 1),
+    ("cmm", 3), ("hx2", 3), ("hmm", 4), ("cmm", 1), ("hz4", 0), ("hmm", 2), ("hx2", 5), ("core", 3),
+    ("cy2", 4), ("core", 1), ("cmm", 2), ("hmm", 3), ("cy2", 0), ("core", 5), ("core", 0), ("hmm", 1),
+    ("cy2", 5), ("hmm", 5), ("cmm", 4), ("hmm", 0), ("silh", 0), ("cmm", 0), ("cmm", 5), ("silc", 0),
+    ("edn", 3), ("fdn", 4), ("fdn", 1), ("edn", 5), ("fx1", 4), ("fdn", 5), ("edn", 4), ("fz1", 1),
+    ("fx1", 5), ("edn", 2), ("fdn", 2), ("e2", 3), ("fx2", 4), ("edn", 1), ("fdn", 0), ("fx2", 5),
+    ("fz2", 1), ("fdn", 3), ("fx1", 2), ("fz1", 0), ("fx1", 3), ("fz3", 1), ("fx2", 2), ("e2", 5), ("e2", 2),
+    ("fx2", 3), ("e2", 4), ("fz2", 0), ("fy1", 5), ("fy1", 4), ("ret", 3), ("fy1", 2), ("ret", 5),
+    ("fz4", 1), ("fy1", 3), ("e2", 1), ("fy2", 5), ("fy2", 4), ("fz3", 0), ("ret", 4), ("fy2", 2),
+    ("fy2", 3), ("ret", 2), ("edn", 0), ("fx1", 1), ("ret", 1), ("fdone", 5), ("comb", 5), ("fz4", 0),
+    ("fdone", 2), ("fdone", 3), ("fdone", 4), ("comb", 4), ("comb", 3), ("fy1", 1), ("e2", 0), ("comb", 2),
+    ("gz2", 5), ("fx1", 0), ("gz2", 4), ("fdone", 1), ("gz2", 3), ("gz2", 2), ("comb", 1), ("ret", 0),
+    ("gz3", 4), ("gz3", 3), ("gz3", 2), ("gz3", 5), ("fy1", 0), ("fdone", 0), ("comb", 0), ("out", 1),
+    ("gz4", 5), ("gz4", 3), ("gz4", 4), ("gz4", 2), ("out", 4), ("out", 5), ("out", 2), ("out", 3),
+    ("out", 0),
 )
 
 
@@ -45,11 +55,10 @@
     xcore = lax.rem(e, 8)
     x = xcore // 2
     c = lax.rem(e, 2)
-    width = tok_ref.shape[1]
-    W = width // CHUNKS
-    NT = W // 256
-    S = W // NZ
-    zcols = pl.ds(pl.multiple_of(z * S, S), S)
+
+    def part_of(j, k):
+        S = WIDTHS[j] // NZ
+        return pl.ds(pl.multiple_of(k * S, S), S)
 
     def add(v, k, n):
         return lax.rem(v + (k + n), n)
@@ -77,12 +86,12 @@
         cp.start()
 
     barrier = pltpu.get_barrier_semaphore()
-    partners = [dev_z(k) for k in range(1, 8)] + [dev_y(1), dev_y(-1)] + [dev_xc(k) for k in range(1, 8)]
+    partners = [dev_z(k) for k in range(1, 8)] + [dev_y(k) for k in range(1, 4)] + [dev_xc(k) for k in range(1, 8)]
     for p in partners:
         pl.semaphore_signal(barrier, inc=1, device_id=p, device_id_type=MESH)
 
     for j in range(CHUNKS):
-        zt[j, z] = tok_ref[:, pl.ds(j * W, W)]
+        zt[j][z] = tok_ref[:, pl.ds(OFFS[j], WIDTHS[j])]
 
     ids = ids_ref[...]
     route = route_ref[...]
@@ -167,6 +176,22 @@
         got((tag, j, "p2"))
         got((tag, j, "m2"))
 
+    def d4_send(tag, j, at, me, dev):
+        for k in (2, 1, 3):
+            send((tag, j, k), at(me, None), at(me, None), dev(k))
+
+    def d4_wait(tag, j):
+        for k in (1, 2, 3):
+            got((tag, j, k))
+
+    def d4_reduce(tag, j, at, slot, me, dev):
+        for k in (2, 1, 3):
+            send((tag, j, k), at(add(me, k, 4), None), slot(k - 1), dev(k))
+
+    def d4_sum(tag, j, at, slot, me):
+        d4_wait(tag, j)
+        tiles(at(me, None), at(me, None), slot(0), slot(1), slot(2))
+
     def r4_first(tag, j, at, slot, me, dev):
         left, right, far = add(me, -1, 4), add(me, 1, 4), add(me, 2, 4)
         send((tag, j, 0), at(far, 0), slot(0), dev(1))
@@ -185,7 +210,7 @@
             summed(dst, *parts)
             return
 
-        @pl.loop(0, NT)
+        @pl.loop(0, dst.shape[-1] // 256, unroll=True)
         def _(n):
             cols = pl.ds(pl.multiple_of(n * 256, 256), 256)
             lead = (slice(None),) * (len(dst.shape) - 1)
@@ -208,27 +233,27 @@
 
     def cold_at(j):
         def at(i, half):
-            return xc_buf.at[j, i] if half is None else xc_buf.at[j, i, pl.ds(4 * half, 4)]
+            return xc_buf[j].at[i] if half is None else xc_buf[j].at[i, pl.ds(4 * half, 4)]
         return at
 
     def hoty_at(j):
         def at(i, half):
             if j in ZLAST:
-                return xh.at[j, c, x, i, :, :, zcols] if half is None else xh.at[j, c, x, i, half, :, zcols]
-            return xh.at[j, c, x, i] if half is None else xh.at[j, c, x, i, half]
+                return xh[j].at[c, x, i, :, :, part_of(j, z)] if half is None else xh[j].at[c, x, i, half, :, part_of(j, z)]
+            return xh[j].at[c, x, i] if half is None else xh[j].at[c, x, i, half]
         return at
 
     def hotx_at(j):
         def at(i, half):
             if j in ZLAST:
                 if half is None:
-                    return xh.at[j, c, i, :, :, :, zcols]
-                return xh.at[j, c, i, pl.ds(2 * half, 2), :, :, zcols]
-            return xh.at[j, c, i] if half is None else xh.at[j, c, i, pl.ds(2 * half, 2)]
+                    return xh[j].at[c, i, :, :, :, part_of(j, z)]
+                return xh[j].at[c, i, pl.ds(2 * half, 2), :, :, part_of(j, z)]
+            return xh[j].at[c, i] if half is None else xh[j].at[c, i, pl.ds(2 * half, 2)]
         return at
 
     def slice_at(j):
-        return lambda k: xh.at[j, c, :, :, :, :, pl.ds(pl.multiple_of(k * S, S), S)]
+        return lambda k: xh[j].at[c, :, :, :, :, part_of(j, k)]
 
     def meta_done():
         both = mt[0]
@@ -264,40 +289,58 @@
         mcomb[3] = (comb - high.astype(F32)).astype(BF)
 
     def d_zstart(j):
-        zg_start("z", lambda s: zt.at[j, s], j, 1)
-        if j == 0:
+        if not copies:
             for k in range(1, NZ):
                 send(("meta", k), mt.at[z], mt.at[z], dev_z(k))
+        if j in ZDIR:
+            for k in (4, 1, 7, 2, 6, 3, 5):
+                send(("z", j, k), zt[j].at[z], zt[j].at[z], dev_z(k))
+        else:
+            zg_start("z", lambda s: zt[j].at[s], j, 1)
 
     def d_zstep(s, j):
         zg_wait("z", j, s - 1)
-        zg_start("z", lambda i: zt.at[j, i], j, s)
+        zg_start("z", lambda i: zt[j].at[i], j, s)
 
     ready = []
+    arrived = []
     started = set()
 
-    def d_select(j):
+    def picked(j, first, groups, row):
         if not ready:
             ready.append(j)
             for k in range(1, NZ):
                 got(("meta", k))
             meta_done()
-        zg_wait("z", j, 4)
-
-        @pl.loop(0, NT)
+        if j not in arrived:
+            arrived.append(j)
+            if j in ZDIR:
+                for k in range(1, NZ):
+                    got(("z", j, k))
+            else:
+                zg_wait("z", j, 4)
+
+        @pl.loop(0, WIDTHS[j] // 256, unroll=True)
         def _(n):
             cols = pl.ds(pl.multiple_of(n * 256, 256), 256)
-            rows = jnp.dot(sel[...], zt[j, :, :, cols].reshape(128, 256), preferred_element_type=F32)
-            xs[j, :, :, cols] = rows.astype(BF).reshape(10, 16, 256)
-
+            rows = jnp.dot(sel[row:row + 16 * groups, :], zt[j][:, :, cols].reshape(128, 256),
+                           preferred_element_type=F32)
+            xs[j][first:first + groups, :, cols] = rows.astype(BF).reshape(groups, 16, 256)
+
+    def d_pickcold(j):
+        picked(j, 0, 8, 0)
         for k in range(1, 8):
-            send(("x", j, k), xs.at[j, lax.rem(xcore + k, 8)], xc_buf.at[j, y, xcore], dev_xc(k))
-        if j in ZLAST:
-            xh[j, c, x, y, :, :, zcols] = xs[j, 8:10, :, zcols]
-        else:
-            xh[j, c, x, y] = xs[j, 8:10]
-        g4_first("hy", j, hoty_at(j), y, dev_y)
-        xc_buf[j, y, xcore] = xs[j, xcore]
+            send(("x", j, k), xs[j].at[lax.rem(xcore + k, 8)], xc_buf[j].at[y, xcore], dev_xc(k))
+        xc_buf[j][y, xcore] = xs[j][xcore]
+
+    def d_pickhot(j):
+        picked(j, 8, 2, 128)
+        if j in ZLAST:
+            xh[j][c, x, y, :, :, part_of(j, z)] = xs[j][8:10, :, part_of(j, z)]
+            d4_send("hy", j, hoty_at(j), y, dev_y)
+        else:
+            xh[j][c, x, y] = xs[j][8:10]
+            g4_first("hy", j, hoty_at(j), y, dev_y)
 
     def d_hoty2(j):
         g4_second("hy", j, hoty_at(j), y, dev_y)
@@ -308,8 +351,12 @@
         g4_first("cy", j, cold_at(j), y, dev_y)
 
     def d_hotx1(j):
-        g4_done("hy", j)
-        g4_first("hx", j, hotx_at(j), x, dev_x)
+        if j in ZLAST:
+            d4_wait("hy", j)
+            d4_send("hx", j, hotx_at(j), x, dev_x)
+        else:
+            g4_done("hy", j)
+            g4_first("hx", j, hotx_at(j), x, dev_x)
 
     def d_coldy2(j):
         g4_second("cy", j, cold_at(j), y, dev_y)
@@ -319,7 +366,7 @@
 
     def d_hotz(s, j):
         if s == 1:
-            g4_done("hx", j)
+            d4_wait("hx", j)
         else:
             zg_wait("hz", j, s - 1)
         zg_start("hz", slice_at(j), j, s)
@@ -328,10 +375,10 @@
         first = block not in started
         started.add(block)
 
-        @pl.loop(0, 3)
+        @pl.loop(0, 3, unroll=True)
         def _(n):
             cols = pl.ds(pl.multiple_of(n * 256, 256), 256)
-            part = jnp.dot(at[...].reshape(512, W), wgu[pl.ds(j * W, W), cols],
+            part = jnp.dot(at[...].reshape(512, WIDTHS[j]), wgu[pl.ds(OFFS[j], WIDTHS[j]), cols],
                            preferred_element_type=F32)
             if first:
                 acc[block, :, cols] = part
@@ -346,23 +393,23 @@
     def d_coldmm(j):
         g4_done("cy", j)
         weights_in()
-        gate_up(j, 0, xc_buf.at[j])
+        gate_up(j, 0, xc_buf[j])
 
     def d_core(j):
         if j in ZLAST:
             zg_wait("hz", j, 4)
         else:
             g4_done("hx", j)
-        send(("core", j), xh.at[j, c], xh.at[j, c], dev_sib)
+        send(("core", j), xh[j].at[c], xh[j].at[c], dev_sib)
 
     def d_hotmm(j):
         got(("core", j))
         weights_in()
-        gate_up(j, 1, xh.at[j, 0])
-        gate_up(j, 2, xh.at[j, 1])
+        gate_up(j, 1, xh[j].at[0])
+        gate_up(j, 2, xh[j].at[1])
 
     def activate(block, masked):
-        @pl.loop(0, 8)
+        @pl.loop(0, 8, unroll=True)
         def _(i):
             rows = pl.ds(pl.multiple_of(i * 64, 64), 64)
             gate = acc[block, rows, 0:384]
@@ -373,10 +420,10 @@
             act[block, rows, :] = value.astype(BF)
 
     def down(j, block, at, shape):
-        @pl.loop(0, NT)
+        @pl.loop(0, WIDTHS[j] // 256, unroll=True)
         def _(n):
             cols = pl.ds(pl.multiple_of(n * 256, 256), 256)
-            wcols = pl.ds(pl.multiple_of(j * W + n * 256, 256), 256)
+            wcols = pl.ds(pl.multiple_of(OFFS[j] + n * 256, 256), 256)
             part = jnp.dot(act[block], wd[:, wcols], preferred_element_type=F32)
             at[(slice(None),) * len(shape) + (cols,)] = part.astype(BF).reshape(shape + (256,))
 
@@ -389,21 +436,21 @@
         activate(2, True)
 
     def ry_at(j):
-        return lambda k: ry.at[j, k]
+        return lambda k: ry[j].at[k]
 
     def rx_at(j):
         if j in ZLAST:
-            return lambda k: rx.at[j, k, :, :, :, pl.ds(0, S)]
-        return lambda k: rx.at[j, k]
+            return lambda k: rx[j].at[k]
+        return lambda k: rx[j].at[k]
 
     def rh_at(j):
         if j in ZLAST:
-            return lambda k: rh.at[j, k, :, pl.ds(0, S)]
-        return lambda k: rh.at[j, k]
+            return lambda k: rh[j].at[k]
+        return lambda k: rh[j].at[k]
 
     def e_down(j):
         sent(lambda key: key[0] == "cy" and key[1] == j)
-        down(j, 0, xc_buf.at[j], (4, 8, 16))
+        down(j, 0, xc_buf[j], (4, 8, 16))
         r4_first("ry", j, cold_at(j), ry_at(j), y, dev_y)
 
     def e_second(j):
@@ -412,19 +459,19 @@
     def e_return(j):
         r4_done("ry", j, cold_at(j), ry_at(j), y)
         for k in range(1, 8):
-            send(("back", j, k), xc_buf.at[j, y, lax.rem(xcore + k, 8)], rr.at[j, xcore], dev_xc(k))
-        rr[j, xcore] = xc_buf[j, y, xcore]
+            send(("back", j, k), xc_buf[j].at[y, lax.rem(xcore + k, 8)], rr[j].at[xcore], dev_xc(k))
+        rr[j][xcore] = xc_buf[j][y, xcore]
 
     def f_down(j):
         sent(lambda key: key[0] in ("hy", "hx", "hz", "core") and key[1] == j)
-        down(j, 1, xh.at[j, 0], (4, 4, 2, 16))
-        down(j, 2, xh.at[j, 1], (4, 4, 2, 16))
-        send(("hcore", j), xh.at[j, 1 - c], hc.at[j], dev_sib)
+        down(j, 1, xh[j].at[0], (4, 4, 2, 16))
+        down(j, 2, xh[j].at[1], (4, 4, 2, 16))
+        send(("hcore", j), xh[j].at[1 - c], hc[j], dev_sib)
 
     def core_sum(j):
         got(("hcore", j))
         for i in range(4):
-            tiles(xh.at[j, c, i], xh.at[j, c, i], hc.at[j, i])
+            tiles(xh[j].at[c, i], xh[j].at[c, i], hc[j].at[i])
 
     def ring_send(tag, j, s, block, slot):
         plus, minus = hops(j)
@@ -447,7 +494,7 @@
                 summed(block(b), block(b), slot(plus + s - 2))
 
     def zh_at(j):
-        return lambda k: zh.at[ZLAST.index(j), k]
+        return lambda k: zh[ZLAST.index(j)].at[k]
 
     def f_z(s, j):
         if s == 1:
@@ -461,50 +508,62 @@
             ring_sum("fz", j, 5, slice_at(j), zh_at(j))
             mine = slice_at(j)(z)
             summed(mine, mine, zh_at(j)(hops(j)[0] - 1), zh_at(j)(6))
+            d4_reduce("rx", j, hotx_at(j), rx_at(j), x, dev_x)
         else:
             core_sum(j)
-        r4_first("rx", j, hotx_at(j), rx_at(j), x, dev_x)
+            r4_first("rx", j, hotx_at(j), rx_at(j), x, dev_x)
 
     def f_x2(j):
         r4_second("rx", j, hotx_at(j), rx_at(j), x, dev_x)
 
     def f_y1(j):
-        r4_done("rx", j, hotx_at(j), rx_at(j), x)
-        r4_first("rh", j, hoty_at(j), rh_at(j), y, dev_y)
+        if j in ZLAST:
+            d4_sum("rx", j, hotx_at(j), rx_at(j), x)
+            d4_reduce("rh", j, hoty_at(j), rh_at(j), y, dev_y)
+        else:
+            r4_done("rx", j, hotx_at(j), rx_at(j), x)
+            r4_first("rh", j, hoty_at(j), rh_at(j), y, dev_y)
 
     def f_y2(j):
         r4_second("rh", j, hoty_at(j), rh_at(j), y, dev_y)
 
     def f_done(j):
-        r4_done("rh", j, hoty_at(j), rh_at(j), y)
+        if j in ZLAST:
+            d4_sum("rh", j, hoty_at(j), rh_at(j), y)
+        else:
+            r4_done("rh", j, hoty_at(j), rh_at(j), y)
 
     def tk_at(j):
-        return lambda k: tk.at[j, k]
+        return lambda k: tk[j].at[k]
 
     def zr_at(j):
-        return lambda k: zr.at[j, k]
+        return lambda k: zr[j].at[k]
 
     def g_combine(j):
         for k in range(1, 8):
             got(("back", j, k))
 
-        @pl.loop(0, NT)
+        @pl.loop(0, WIDTHS[j] // 256, unroll=True)
         def _(n):
             cols = pl.ds(pl.multiple_of(n * 256, 256), 256)
-            cold = rr[j, :, :, cols].reshape(128, 256)
+            cold = rr[j][:, :, cols].reshape(128, 256)
             total = jnp.dot(mcomb[0], cold, preferred_element_type=F32)
             total += jnp.dot(mcomb[1], cold, preferred_element_type=F32)
             if j not in ZLAST:
-                total += hot_part(xh[j, c, x, y, :, :, cols].reshape(32, 256))
-            tk[j, :, :, cols] = total.astype(BF).reshape(8, 16, 256)
-
-        if j in ZLAST:
-            cold = rr[j, :, :, zcols].reshape(128, S)
+                total += hot_part(xh[j][c, x, y, :, :, cols].reshape(32, 256))
+            tk[j][:, :, cols] = total.astype(BF).reshape(8, 16, 256)
+
+        if j in ZLAST:
+            cold = rr[j][:, :, part_of(j, z)].reshape(128, WIDTHS[j] // NZ)
             total = jnp.dot(mcomb[0], cold, preferred_element_type=F32)
             total += jnp.dot(mcomb[1], cold, preferred_element_type=F32)
-            total += hot_part(xh[j, c, x, y, :, :, zcols].reshape(32, S))
-            tk[j, :, :, zcols] = total.astype(BF).reshape(8, 16, S)
-        ring_send("rz", j, 1, tk_at(j), zr_at(j))
+            total += hot_part(xh[j][c, x, y, :, :, part_of(j, z)].reshape(32, WIDTHS[j] // NZ))
+            tk[j][:, :, part_of(j, z)] = total.astype(BF).reshape(8, 16, WIDTHS[j] // NZ)
+        if j in RDIR:
+            for k in (4, 1, 7, 2, 6, 3, 5):
+                send(("rz", j, k), tk[j].at[add(z, k, NZ)], zr[j].at[k - 1], dev_z(k))
+        else:
+            ring_send("rz", j, 1, tk_at(j), zr_at(j))
 
     def hot_part(rows):
         total = jnp.dot(mcomb[2][:, 0:32], rows, preferred_element_type=F32)
@@ -515,14 +574,19 @@
         ring_send("rz", j, s, tk_at(j), zr_at(j))
 
     def g_out(j):
+        if j in RDIR:
+            for k in range(1, NZ):
+                got(("rz", j, k))
+            summed(out_ref.at[:, pl.ds(OFFS[j], WIDTHS[j])], tk[j].at[z], *[zr[j].at[k] for k in range(7)])
+            return
         ring_sum("rz", j, 5, tk_at(j), zr_at(j))
-        summed(out_ref.at[:, pl.ds(j * W, W)], tk.at[j, z], zr.at[j, hops(j)[0] - 1], zr.at[j, 6])
+        summed(out_ref.at[:, pl.ds(OFFS[j], WIDTHS[j])], tk[j].at[z], zr[j].at[hops(j)[0] - 1], zr[j].at[6])
 
     def stepped(f):
         return [functools.partial(f, s) for s in range(1, 5)]
 
     steps = {
-        "z1": d_zstart, "sel": d_select, "hy2": d_hoty2, "hx1": d_hotx1, "hx2": d_hotx2, "core": d_core,
+        "z1": d_zstart, "selc": d_pickcold, "selh": d_pickhot, "hy2": d_hoty2, "hx1": d_hotx1, "hx2": d_hotx2, "core": d_core,
         "cy1": d_coldy1, "cy2": d_coldy2, "cmm": d_coldmm, "hmm": d_hotmm, "silc": silu_cold,
         "silh": silu_hot, "edn": e_down, "e2": e_second, "ret": e_return, "fdn": f_down, "fx1": f_x1,
         "fx2": f_x2, "fy1": f_y1, "fy2": f_y2, "fdone": f_done, "comb": g_combine, "out": g_out,
@@ -537,33 +601,38 @@
 
 def local(hidden_states, expert_ids, route_weights, w_gate, w_up, w_down):
     rows, width = hidden_states.shape
-    W = width // CHUNKS
     vmem = pl.BlockSpec(memory_space=pltpu.VMEM)
     hbm = pl.BlockSpec(memory_space=pl.ANY)
-    C = CHUNKS
+
+    def each(*shape):
+        return [pltpu.VMEM(shape + (w,), BF) for w in WIDTHS]
+
+    def slots(full, part):
+        return [pltpu.VMEM(part + (w // NZ,) if j in ZLAST else full + (w,), BF) for j, w in enumerate(WIDTHS)]
+
     scratch = [
-        pltpu.VMEM((C, 8, 16, W), BF),
+        each(8, 16),
         pltpu.VMEM((8, 16, 128), F32),
-        pltpu.VMEM((C, 10, 16, W), BF),
-        pltpu.VMEM((C, 4, 8, 16, W), BF),
-        pltpu.VMEM((C, 2, 4, 4, 2, 16, W), BF),
+        each(10, 16),
+        each(4, 8, 16),
+        each(2, 4, 4, 2, 16),
         pltpu.VMEM((width, 768), BF),
         pltpu.VMEM((384, width), BF),
         pltpu.VMEM((3, 512, 768), F32),
         pltpu.VMEM((3, 512, 384), BF),
-        pltpu.VMEM((C, 6, 4, 16, W), BF),
-        pltpu.VMEM((C, 4, 4, 2, 16, W), BF),
-        pltpu.VMEM((C, 6, 2, 2, 16, W), BF),
-        pltpu.VMEM((C, 6, 16, W), BF),
-        pltpu.VMEM((C, 8, 16, W), BF),
-        pltpu.VMEM((C, 8, 16, W), BF),
-        pltpu.VMEM((C, 7, 16, W), BF),
-        pltpu.VMEM((len(ZLAST), 7, 4, 4, 2, 16, W // NZ), BF),
+        each(6, 4, 16),
+        each(4, 4, 2, 16),
+        slots((6, 2, 2, 16), (3, 4, 2, 16)),
+        slots((6, 16), (3, 2, 16)),
+        each(8, 16),
+        each(8, 16),
+        each(7, 16),
+        [pltpu.VMEM((7, 4, 4, 2, 16, WIDTHS[j] // NZ), BF) for j in ZLAST],
         pltpu.VMEM((8, 128), F32),
         pltpu.VMEM((160, 128), BF),
         pltpu.VMEM((4, 128, 128), BF),
-        pltpu.SemaphoreType.DMA((C * NSEM + 8,)),
-        pltpu.SemaphoreType.DMA((C * NSEM + 8,)),
+        pltpu.SemaphoreType.DMA((CHUNKS * NSEM + 8,)),
+        pltpu.SemaphoreType.DMA((CHUNKS * NSEM + 8,)),
         pltpu.SemaphoreType.DMA((3,)),
     ]
     return pl.pallas_call(

time: 154 us -> 136 us (0.88)
  Pallas kernels: 152 us -> 133 us
    pallas_call x1, Pallas kernels: 152 us -> 133 us  [local(): pl.pallas_call(kernel, out_shape=jax.ShapeDtypeStruct((rows, width), BF),...]
where the time goes in v3:
time: 136 us; the launch traced here: 135 us
  Pallas kernels  133 us (98%)
  local copies, waits for them, and re-layouts  1.57 us (1%)
    pallas_call x1, Pallas kernels, local(): pl.pallas_call(kernel, out_shape=jax.ShapeDtypeStruct((rows, width), BF),...  133 us

profile of v3, /device:TPU:2, one launch (start us, length us, event | category | flops | bytes accessed | tf_op | source)
XLA Modules:
  0.0 134.7 jit_solution(151679330121597945)
XLA Ops:
  0.0 133.1 %shard_map.64 = bf16[16,4096]{1,0:T(8,128)(2,1)} custom-call(bf16[16,4096]{1,0:T(8,128)(2,1)} %tok_ref.1, s32[8,16]{1,0:T(8,128)} %bitcast.2, f32[8,16]{1,0:T(8,128)} %bitcast.3, bf16[1,4096,384]{2,1,0:T(8,128)(2,1)} %wg_hbm.1, bf16[1,4096,384]{2,1,0:T(8,128)(2,1)} %wu_hbm.1, bf16[1,384,4096]{2,1,0:T(8,128)(2,1)} %wd_hbm.1), custom_call_target="tpu_custom_call" | custom-call | tf_op jit(solution)/shard_map/pallas_call | solution.py:638
  133.1 1.6 %copy.8 = bf16[16,4096]{1,0:T(8,128)(2,1)} copy(bf16[16,4096]{1,0:T(8,128)(2,1)} %shard_map.64) | data formatting | bytes 262144
